TPU v7x, 32 devices: a whole 2x2x4 slice. The times are simulated.
32 devices in a mesh: cell: 4 (over y, x), chan: 8 (over z, core).
Axes of the slice: x: 2, y: 2, z: 4, core: 2. Of those that a mesh axis runs over, the one named last changes fastest.
Arguments:
- slab: bfloat16 [32768, 8192], P('cell', 'chan'), may hold values from -6 to 6
- cell_factor: float32 [32, 32768], P(None, 'cell'), may hold values from -6 to 6
- chan_factor: float32 [32, 8192], P(None, 'chan'), may hold values from -6 to 6
- cell_mttkrp: float32 [32, 32768], P(None, 'cell'), may hold values from -12 to 12
- chan_mttkrp: float32 [32, 8192], P(None, 'chan'), may hold values from -12 to 12
- cell_gram_acc: float32 [32, 32], replicated, as said below
- chan_gram_acc: float32 [32, 32], replicated, as said below
Outputs:
- time_row: float32 [32], replicated
- new_cell_factor: float32 [32, 32768], P(None, 'cell')
- new_chan_factor: float32 [32, 8192], P(None, 'chan')
- new_cell_mttkrp: float32 [32, 32768], P(None, 'cell')
- new_chan_mttkrp: float32 [32, 8192], P(None, 'chan')
- new_cell_gram: float32 [32, 32], replicated
- new_chan_gram: float32 [32, 32], replicated
Inputs may be any that keep to these rules, and one draw needn't show every extreme that they name: `cell_gram_acc`: symmetric with a dominant positive diagonal. `chan_gram_acc`: symmetric with a dominant positive diagonal.
All inputs are finite; a program needn't handle non-finite values.
Results may differ from a plain program's by a relative error of at most 0.0033.
Values sent between devices are 32-bit elements; how exact they have to be, the bound alone decides.
No kernel may reach another device: no remote copies, remote signals or barrier semaphores. Data moves between devices by JAX's collectives and lax.ppermute only.
A program may use at most 64 MiB of HBM per device.

v0:
```python
import math
import jax
import jax.numpy as jnp
from jax import lax
from jax.sharding import PartitionSpec as P


def spd_solve(matrix, right):
    lower = jnp.linalg.cholesky(matrix)
    return jax.scipy.linalg.cho_solve((lower, True), right)


def body(slab, cell_factor, chan_factor, cell_mttkrp, chan_mttkrp, cell_gram_acc, chan_gram_acc):
    hi = lax.Precision.HIGHEST
    n_cell = lax.axis_size("cell")
    n_chan = lax.axis_size("chan")
    local_rows = slab.shape[0]
    local_cols = slab.shape[1]
    all_rows = local_rows * n_cell
    all_cols = local_cols * n_chan
    chan_low = chan_factor.astype(jnp.bfloat16)
    slab_chan = lax.dot_general(
        chan_low, slab, (((1,), (1,)), ((), ())), preferred_element_type=jnp.float32
    )
    rhs_part = jnp.sum(cell_factor * slab_chan, axis=1) / math.sqrt(all_rows * all_cols)
    cell_part = jnp.dot(cell_factor, cell_factor.T, precision=hi) / all_rows
    chan_part = jnp.dot(chan_factor, chan_factor.T, precision=hi) / all_cols
    rhs = lax.psum(rhs_part, ("cell", "chan"))
    cell_norm = lax.psum(cell_part, "cell")
    chan_norm = lax.psum(chan_part, "chan")
    time_row = spd_solve(cell_norm * chan_norm, rhs[:, None])[:, 0]
    outer = time_row[:, None] * time_row[None, :]
    new_cell_gram = cell_gram_acc + chan_norm * outer
    summed = lax.psum(slab_chan, "chan")
    new_cell_mttkrp = cell_mttkrp + time_row[:, None] * summed / math.sqrt(all_cols)
    new_cell_factor = spd_solve(new_cell_gram, new_cell_mttkrp)
    local_gram = jnp.dot(new_cell_factor, new_cell_factor.T, precision=hi) / all_rows
    new_norm = lax.psum(local_gram, "cell")
    cell_low = new_cell_factor.astype(jnp.bfloat16)
    slab_cell = jnp.dot(cell_low, slab, preferred_element_type=jnp.float32)
    cell_summed = lax.psum(slab_cell, "cell")
    new_chan_mttkrp = chan_mttkrp + time_row[:, None] * cell_summed / math.sqrt(all_rows)
    new_chan_gram = chan_gram_acc + new_norm * outer
    new_chan_factor = spd_solve(new_chan_gram, new_chan_mttkrp)
    return (
        time_row,
        new_cell_factor,
        new_chan_factor,
        new_cell_mttkrp,
        new_chan_mttkrp,
        new_cell_gram,
        new_chan_gram,
    )


def solution(mesh):
    placed = (
        P("cell", "chan"),
        P(None, "cell"),
        P(None, "chan"),
        P(None, "cell"),
        P(None, "chan"),
        P(),
        P(),
    )
    return jax.shard_map(
        body,
        mesh=mesh,
        in_specs=placed,
        out_specs=(
            P(),
            P(None, "cell"),
            P(None, "chan"),
            P(None, "cell"),
            P(None, "chan"),
            P(),
            P(),
        ),
        check_vma=False,
    )
```

profile of v0, /device:TPU:0, one launch (start us, length us, event | category | flops | bytes accessed | tf_op | source)
XLA Modules:
  0.0 202.9 jit_solution(13627783786792271417)
XLA Ops:
  7.3 12.4 %multiply_reduce_fusion = (f32[32]{0:T(128)S(1)}, f32[32,8192]{1,0:T(8,128)}) fusion(f32[32,8192]{1,0:T(8,128)} %param.9, bf16[8192,1024]{1,0:T(8,128)(2,1)} %param.8, f32[32,1024]{1,0:T(8,128)} %param.10), kind=kOutput, calls=%fused_computation.6 | convolution fusion | flops 537427968 | bytes 19005568 | tf_op jit(solution)/shard_map/dot_general | solution.py:22
  20.0 1.0 convolution_multiply_fusion.2
  21.0 30.4 %psum.43 = f32[32,32]{0,1:T(8,128)S(1)} all-reduce(f32[32,32]{0,1:T(8,128)S(1)} %convolution_multiply_fusion.1), channel_id=1, replica_groups=mesh['cell'=4,'chan'=8] {'chan'}, use_global_device_ids=true, to_apply=%region_1.0 | all-reduce | flops 1024 | bytes 8192 | tf_op jit(solution)/shard_map/psum | solution.py:30
  51.3 16.0 %psum.42 = f32[32,32]{0,1:T(8,128)S(1)} all-reduce(f32[32,32]{0,1:T(8,128)S(1)} %convolution_multiply_fusion.2), channel_id=1, replica_groups=mesh['cell'=4,'chan'=8] {'cell'}, use_global_device_ids=true, to_apply=%region_0.0 | all-reduce | flops 1024 | bytes 8192 | tf_op jit(solution)/shard_map/psum | solution.py:29
  67.4 2.9 %cholesky.59 = f32[32,32]{1,0:T(8,128)S(1)} custom-call(f32[32,32]{1,0:T(8,128)S(1)} %fusion.21), custom_call_target="Cholesky" | custom-call | tf_op jit(solution)/shard_map/jit(cholesky)/cholesky | solution.py:9
  70.4 0.6 compare_reduce_fusion.2
  71.0 0.7 fusion.4
  71.7 2.4 %custom-call.23 = f32[1,32,32]{1,2,0:T(8,128)S(1)} custom-call(f32[1,32,32]{2,1,0:T(8,128)S(1)} %fusion.4), custom_call_target="InvertDiagBlocksLowerTriangular" | custom-call | tf_op jit(solution)/shard_map/jit(_cho_solve)/triangular_solve | solution.py:10
  74.1 37.0 %psum.44 = f32[32]{0:T(128)S(1)} all-reduce(f32[32]{0:T(128)S(1)} %broadcast_multiply_fusion), channel_id=1, replica_groups=mesh['cell'=4,'chan'=8] {'cell','chan'}, use_global_device_ids=true, to_apply=%region_5.7 | all-reduce | flops 32 | bytes 256 | tf_op jit(solution)/shard_map/psum | solution.py:28
  111.7 2.9 %cholesky.70 = f32[32,32]{1,0:T(8,128)S(1)} custom-call(f32[32,32]{1,0:T(8,128)S(1)} %fusion.18), custom_call_target="Cholesky" | custom-call | tf_op jit(solution)/shard_map/jit(cholesky)/cholesky | solution.py:9
  115.3 0.7 fusion.5
  116.0 2.4 %custom-call.24 = f32[1,32,32]{1,2,0:T(8,128)S(1)} custom-call(f32[1,32,32]{2,1,0:T(8,128)S(1)} %fusion.5), custom_call_target="InvertDiagBlocksLowerTriangular" | custom-call | tf_op jit(solution)/shard_map/jit(_cho_solve)/triangular_solve | solution.py:10
  118.5 1.4 multiply_add_fusion
  119.9 1.0 fusion.16
  121.0 1.0 fusion.14
  122.0 1.0 convolution_multiply_fusion
  123.0 9.4 %fusion = f32[32,1024]{1,0:T(8,128)} fusion(bf16[8192,1024]{1,0:T(8,128)(2,1)} %param.8, f32[32,8192]{1,0:T(8,128)S(1)} %fusion.14), kind=kOutput, calls=%fused_computation.7 | convolution fusion | flops 537133056 | bytes 17956864 | tf_op jit(solution)/shard_map/dot_general | solution.py:40
  132.4 15.9 %psum.46 = f32[32,32]{0,1:T(8,128)S(1)} all-reduce(f32[32,32]{0,1:T(8,128)S(1)} %convolution_multiply_fusion), channel_id=1, replica_groups=mesh['cell'=4,'chan'=8] {'cell'}, use_global_device_ids=true, to_apply=%region_7.9 | all-reduce | flops 1024 | bytes 8192 | tf_op jit(solution)/shard_map/psum | solution.py:38
  148.5 2.9 %cholesky.81 = f32[32,32]{1,0:T(8,128)S(1)} custom-call(f32[32,32]{1,0:T(8,128)S(1)} %fusion.13), custom_call_target="Cholesky" | custom-call | tf_op jit(solution)/shard_map/jit(cholesky)/cholesky | solution.py:9
  152.1 0.7 fusion.6
  152.8 2.4 %custom-call.25 = f32[1,32,32]{1,2,0:T(8,128)S(1)} custom-call(f32[1,32,32]{2,1,0:T(8,128)S(1)} %fusion.6), custom_call_target="InvertDiagBlocksLowerTriangular" | custom-call | tf_op jit(solution)/shard_map/jit(_cho_solve)/triangular_solve | solution.py:10
  155.2 38.6 %all-reduce.5.cloned.1.call-done = f32[32,1024]{1,0:T(8,128)} async-done(((f32[32,1024]{1,0:T(8,128)}), f32[32,1024]{1,0:T(8,128)}) %all-reduce.5.cloned.1.call-update) | async-done | bytes 131088 | tf_op jit(solution)/shard_map/psum | solution.py:41
  193.8 1.0 multiply_add_fusion.1
  195.1 0.9 fusion.9
  (50 shorter events, 3.0 us)
Async XLA Ops:
  7.2 12.5 %copy-start.3 = (f32[32,1024]{1,0:T(8,128)S(1)}, f32[32,1024]{1,0:T(8,128)}, u32[]{:S(2)}) copy-start(f32[32,1024]{1,0:T(8,128)} %param.10) | copy-start | bytes 393220
  7.2 12.8 %copy-start.1 = (f32[32,8192]{1,0:T(8,128)S(1)}, f32[32,8192]{1,0:T(8,128)}, u32[]{:S(2)}) copy-start(f32[32,8192]{1,0:T(8,128)} %param.9) | copy-start | bytes 3145732
  7.2 104.3 %copy-start.10 = (f32[32,32]{1,0:T(8,128)S(1)}, f32[32,32]{1,0:T(8,128)}, u32[]{:S(2)}) copy-start(f32[32,32]{1,0:T(8,128)} %param.13) | copy-start | bytes 12292
  7.2 111.2 %copy-start.11 = (f32[32,32]{1,0:T(8,128)S(1)}, f32[32,32]{1,0:T(8,128)}, u32[]{:S(2)}) copy-start(f32[32,32]{1,0:T(8,128)} %param.14) | copy-start | bytes 12292
  7.2 111.3 %copy-start.4 = (f32[32,8192]{1,0:T(8,128)S(1)}, f32[32,8192]{1,0:T(8,128)}, u32[]{:S(2)}) copy-start(f32[32,8192]{1,0:T(8,128)} %param.11) | copy-start | bytes 3145732
  7.2 111.3 %all-reduce.3.cloned.1.call-start = ((), (), s32[]{:S(2)}) async-start(), calls=%async_computation | async-start | bytes 2097152 | tf_op jit(solution)/shard_map/psum | solution.py:34
  19.7 174.2 %all-reduce.5.cloned.1.call-start = ((), (), s32[]{:S(2)}) async-start(), calls=%async_computation.1 | async-start | bytes 262144 | tf_op jit(solution)/shard_map/psum | solution.py:41
  111.5 82.4 %copy-start.9 = (f32[32]{0:T(128)}, f32[32]{0:T(128)S(1)}, u32[]{:S(2)}) copy-start(f32[32]{0:T(128)S(1)} %convolution_bitcast_fusion) | copy-start | bytes 388
  111.7 20.7 %copy-start.7 = (f32[32,32]{1,0:T(8,128)}, f32[32,32]{1,0:T(8,128)S(1)}, u32[]{:S(2)}) copy-start(f32[32,32]{1,0:T(8,128)S(1)} %copy.18) | copy-start | bytes 12292
  119.9 32.8 %copy-start.2 = (f32[32,8192]{1,0:T(8,128)}, f32[32,8192]{1,0:T(8,128)S(1)}, u32[]{:S(2)}) copy-start(f32[32,8192]{1,0:T(8,128)S(1)} %multiply_add_fusion) | copy-start | bytes 3145732
  119.9 73.9 %copy-start.6 = (f32[32,1024]{1,0:T(8,128)S(1)}, f32[32,1024]{1,0:T(8,128)}, u32[]{:S(2)}) copy-start(f32[32,1024]{1,0:T(8,128)} %param.12) | copy-start | bytes 393220
  122.0 74.1 %copy-start = (f32[32,8192]{1,0:T(8,128)}, f32[32,8192]{1,0:T(8,128)S(1)}, u32[]{:S(2)}) copy-start(f32[32,8192]{1,0:T(8,128)S(1)} %fusion.14) | copy-start | bytes 3145732
  148.5 47.6 %copy-start.8 = (f32[32,32]{1,0:T(8,128)}, f32[32,32]{1,0:T(8,128)S(1)}, u32[]{:S(2)}) copy-start(f32[32,32]{1,0:T(8,128)S(1)} %copy.21) | copy-start | bytes 12292
  194.8 1.3 copy-start.5
Sparse Core Ops, SparseCore 0:
  19.8 61.7 all-reduce.2
  152.2 41.5 all-reduce.4
where the time goes:
time: 203 us
  blocking collectives  99.3 us (49%)
  waiting for transfers between devices  38.7 us (19%)
  matrix products  27.5 us (14%)
  other arithmetic  22.6 us (11%)
  between operations  14.3 us (7%)
    psum x1, waiting for transfers between devices, body(): cell_summed = lax.psum(slab_cell, 'cell')  38.6 us
    psum x1, blocking collectives, body(): rhs = lax.psum(rhs_part, ('cell', 'chan'))  37 us
    psum x1, blocking collectives, body(): chan_norm = lax.psum(chan_part, 'chan')  30.4 us
    psum x1, blocking collectives, body(): cell_norm = lax.psum(cell_part, 'cell')  16 us
    psum x1, blocking collectives, body(): new_norm = lax.psum(local_gram, 'cell')  15.9 us
    dot_general x1, matrix products, body(): lax.dot_general(chan_low, slab, (((1,), (1,)), ((), ())), preferred_eleme...  12.4 us
    another operation x9, other arithmetic, spd_solve(): lower = jnp.linalg.cholesky(matrix)  10.8 us
    dot_general x1, matrix products, body(): slab_cell = jnp.dot(cell_low, slab, preferred_element_type=jnp.float32)  9.41 us
  transfers between devices with their start and end apart: 2, of which 1 were waited for; matrix products, arithmetic and copies ran while one was open for 9% of the time, Pallas kernels for 0%

commit v1 on v0

--- a/solution.py
+++ b/solution.py
@@ -3,6 +3,12 @@
 import jax.numpy as jnp
 from jax import lax
 from jax.sharding import PartitionSpec as P
+
+
+def get_terms_up(x_part):
+    for b in ("chan", "cell"):
+        x_part = lax.psum(x_part, b)
+    return x_part
 
 
 def spd_solve(matrix, right):
@@ -25,7 +31,7 @@
     rhs_part = jnp.sum(cell_factor * slab_chan, axis=1) / math.sqrt(all_rows * all_cols)
     cell_part = jnp.dot(cell_factor, cell_factor.T, precision=hi) / all_rows
     chan_part = jnp.dot(chan_factor, chan_factor.T, precision=hi) / all_cols
-    rhs = lax.psum(rhs_part, ("cell", "chan"))
+    rhs = get_terms_up(rhs_part)
     cell_norm = lax.psum(cell_part, "cell")
     chan_norm = lax.psum(chan_part, "chan")
     time_row = spd_solve(cell_norm * chan_norm, rhs[:, None])[:, 0]

time: 203 us -> 164 us (0.81)
  blocking collectives: 99.3 us -> 62.1 us
    psum x1 -> x0, blocking collectives: 37 us -> none  [body(): rhs = lax.psum(rhs_part, ('cell', 'chan'))]
  transfers between devices with their start and end apart: 2 -> 2, of which waited for: 1 -> 2; matrix products, arithmetic and copies ran while one was open for 9% -> 11% of each run, Pallas kernels for 0% -> 0%
where the time goes in v1:
time: 164 us
  blocking collectives  62.1 us (38%)
  waiting for transfers between devices  36.9 us (22%)
  matrix products  27.5 us (17%)
  other arithmetic  22.6 us (14%)
  between operations  14.3 us (9%)
    psum x1, waiting for transfers between devices, body(): cell_summed = lax.psum(slab_cell, 'cell')  36.6 us
    psum x1, blocking collectives, body(): chan_norm = lax.psum(chan_part, 'chan')  30.3 us
    psum x1, blocking collectives, body(): cell_norm = lax.psum(cell_part, 'cell')  16.2 us
    psum x1, blocking collectives, body(): new_norm = lax.psum(local_gram, 'cell')  15.5 us
    dot_general x1, matrix products, body(): lax.dot_general(chan_low, slab, (((1,), (1,)), ((), ())), preferred_eleme...  12.4 us
    another operation x9, other arithmetic, spd_solve(): lower = jnp.linalg.cholesky(matrix)  10.8 us
    dot_general x1, matrix products, body(): slab_cell = jnp.dot(cell_low, slab, preferred_element_type=jnp.float32)  9.41 us
    another operation x6, other arithmetic, spd_solve(): return jax.scipy.linalg.cho_solve((lower, True), right)  9.29 us
  transfers between devices with their start and end apart: 2, of which 2 were waited for; matrix products, arithmetic and copies ran while one was open for 11% of the time, Pallas kernels for 0%

profile of v1, /device:TPU:0, one launch (start us, length us, event | category | flops | bytes accessed | tf_op | source)
XLA Modules:
  0.0 163.9 jit_solution(3250509162322635334)
XLA Ops:
  7.3 12.4 %multiply_reduce_fusion = (f32[32]{0:T(128)S(1)}, f32[32,8192]{1,0:T(8,128)}) fusion(f32[32,8192]{1,0:T(8,128)} %param.9, bf16[8192,1024]{1,0:T(8,128)(2,1)} %param.8, f32[32,1024]{1,0:T(8,128)} %param.10), kind=kOutput, calls=%fused_computation.6 | convolution fusion | flops 537427968 | bytes 19005568 | tf_op jit(solution)/shard_map/dot_general | solution.py:28
  20.0 1.0 convolution_multiply_fusion.2
  21.0 30.3 %all-reduce = (f32[32,32]{0,1:T(8,128)S(1)}, f32[32]{0:T(128)S(1)}) all-reduce(f32[32,32]{0,1:T(8,128)S(1)} %convolution_multiply_fusion.1, f32[32]{0:T(128)S(1)} %broadcast_multiply_fusion), channel_id=1, replica_groups=mesh['cell'=4,'chan'=8] {'chan'}, use_global_device_ids=true, to_apply=%region_1.0 | all-reduce | flops 1056 | bytes 8448 | tf_op jit(solution)/shard_map/psum | solution.py:36
  51.3 16.2 %all-reduce.1 = (f32[32,32]{0,1:T(8,128)S(1)}, f32[32]{0:T(128)S(1)}) all-reduce(f32[32,32]{0,1:T(8,128)S(1)} %convolution_multiply_fusion.2, f32[32]{0:T(128)S(1)} %get-tuple-element.16), channel_id=1, replica_groups=mesh['cell'=4,'chan'=8] {'cell'}, use_global_device_ids=true, to_apply=%region_0.0 | all-reduce | flops 1056 | bytes 8448 | tf_op jit(solution)/shard_map/psum | solution.py:35
  67.6 2.9 %cholesky.59 = f32[32,32]{1,0:T(8,128)S(1)} custom-call(f32[32,32]{1,0:T(8,128)S(1)} %fusion.21), custom_call_target="Cholesky" | custom-call | tf_op jit(solution)/shard_map/jit(cholesky)/cholesky | solution.py:15
  70.6 0.6 compare_reduce_fusion.2
  71.2 0.7 fusion.4
  71.9 2.4 %custom-call.23 = f32[1,32,32]{1,2,0:T(8,128)S(1)} custom-call(f32[1,32,32]{2,1,0:T(8,128)S(1)} %fusion.4), custom_call_target="InvertDiagBlocksLowerTriangular" | custom-call | tf_op jit(solution)/shard_map/jit(_cho_solve)/triangular_solve | solution.py:16
  74.9 2.9 %cholesky.70 = f32[32,32]{1,0:T(8,128)S(1)} custom-call(f32[32,32]{1,0:T(8,128)S(1)} %fusion.18), custom_call_target="Cholesky" | custom-call | tf_op jit(solution)/shard_map/jit(cholesky)/cholesky | solution.py:15
  77.8 0.6 compare_reduce_fusion.1
  78.5 0.7 fusion.5
  79.1 2.5 %custom-call.24 = f32[1,32,32]{1,2,0:T(8,128)S(1)} custom-call(f32[1,32,32]{2,1,0:T(8,128)S(1)} %fusion.5), custom_call_target="InvertDiagBlocksLowerTriangular" | custom-call | tf_op jit(solution)/shard_map/jit(_cho_solve)/triangular_solve | solution.py:16
  81.9 1.4 multiply_add_fusion
  83.4 1.0 fusion.16
  84.4 1.0 fusion.14
  85.4 1.0 convolution_multiply_fusion
  86.4 9.4 %fusion = f32[32,1024]{1,0:T(8,128)} fusion(bf16[8192,1024]{1,0:T(8,128)(2,1)} %param.8, f32[32,8192]{1,0:T(8,128)S(1)} %fusion.14), kind=kOutput, calls=%fused_computation.7 | convolution fusion | flops 537133056 | bytes 17956864 | tf_op jit(solution)/shard_map/dot_general | solution.py:46
  95.8 15.5 %psum.54 = f32[32,32]{0,1:T(8,128)S(1)} all-reduce(f32[32,32]{0,1:T(8,128)S(1)} %convolution_multiply_fusion), channel_id=1, replica_groups=mesh['cell'=4,'chan'=8] {'cell'}, use_global_device_ids=true, to_apply=%region_8.10 | all-reduce | flops 1024 | bytes 8192 | tf_op jit(solution)/shard_map/psum | solution.py:44
  111.5 2.9 %cholesky.81 = f32[32,32]{1,0:T(8,128)S(1)} custom-call(f32[32,32]{1,0:T(8,128)S(1)} %fusion.13), custom_call_target="Cholesky" | custom-call | tf_op jit(solution)/shard_map/jit(cholesky)/cholesky | solution.py:15
  115.1 0.7 fusion.6
  115.8 2.4 %custom-call.25 = f32[1,32,32]{1,2,0:T(8,128)S(1)} custom-call(f32[1,32,32]{2,1,0:T(8,128)S(1)} %fusion.6), custom_call_target="InvertDiagBlocksLowerTriangular" | custom-call | tf_op jit(solution)/shard_map/jit(_cho_solve)/triangular_solve | solution.py:16
  118.2 36.6 %all-reduce.7.cloned.1.call-done = f32[32,1024]{1,0:T(8,128)} async-done(((f32[32,1024]{1,0:T(8,128)}), f32[32,1024]{1,0:T(8,128)}) %all-reduce.7.cloned.1.call-update) | async-done | bytes 131088 | tf_op jit(solution)/shard_map/psum | solution.py:47
  154.9 1.0 multiply_add_fusion.1
  156.2 0.9 fusion.9
  (49 shorter events, 2.6 us)
Async XLA Ops:
  7.2 12.5 %copy-start.3 = (f32[32,1024]{1,0:T(8,128)S(1)}, f32[32,1024]{1,0:T(8,128)}, u32[]{:S(2)}) copy-start(f32[32,1024]{1,0:T(8,128)} %param.10) | copy-start | bytes 393220
  7.2 12.8 %copy-start.1 = (f32[32,8192]{1,0:T(8,128)S(1)}, f32[32,8192]{1,0:T(8,128)}, u32[]{:S(2)}) copy-start(f32[32,8192]{1,0:T(8,128)} %param.9) | copy-start | bytes 3145732
  7.2 67.4 %copy-start.10 = (f32[32,32]{1,0:T(8,128)S(1)}, f32[32,32]{1,0:T(8,128)}, u32[]{:S(2)}) copy-start(f32[32,32]{1,0:T(8,128)} %param.13) | copy-start | bytes 12292
  7.2 74.4 %copy-start.11 = (f32[32,32]{1,0:T(8,128)S(1)}, f32[32,32]{1,0:T(8,128)}, u32[]{:S(2)}) copy-start(f32[32,32]{1,0:T(8,128)} %param.14) | copy-start | bytes 12292
  7.2 74.7 %copy-start.4 = (f32[32,8192]{1,0:T(8,128)S(1)}, f32[32,8192]{1,0:T(8,128)}, u32[]{:S(2)}) copy-start(f32[32,8192]{1,0:T(8,128)} %param.11) | copy-start | bytes 3145732
  7.2 74.7 %all-reduce.5.cloned.1.call-start = ((), (), s32[]{:S(2)}) async-start(), calls=%async_computation | async-start | bytes 2097152 | tf_op jit(solution)/shard_map/psum | solution.py:40
  19.7 135.2 %all-reduce.7.cloned.1.call-start = ((), (), s32[]{:S(2)}) async-start(), calls=%async_computation.1 | async-start | bytes 262144 | tf_op jit(solution)/shard_map/psum | solution.py:47
  74.6 80.2 %copy-start.9 = (f32[32]{0:T(128)}, f32[32]{0:T(128)S(1)}, u32[]{:S(2)}) copy-start(f32[32]{0:T(128)S(1)} %convolution_bitcast_fusion) | copy-start | bytes 388
  74.8 21.0 %copy-start.7 = (f32[32,32]{1,0:T(8,128)}, f32[32,32]{1,0:T(8,128)S(1)}, u32[]{:S(2)}) copy-start(f32[32,32]{1,0:T(8,128)S(1)} %copy.18) | copy-start | bytes 12292
  83.3 32.5 %copy-start.2 = (f32[32,8192]{1,0:T(8,128)}, f32[32,8192]{1,0:T(8,128)S(1)}, u32[]{:S(2)}) copy-start(f32[32,8192]{1,0:T(8,128)S(1)} %multiply_add_fusion) | copy-start | bytes 3145732
  83.3 71.5 %copy-start.6 = (f32[32,1024]{1,0:T(8,128)S(1)}, f32[32,1024]{1,0:T(8,128)}, u32[]{:S(2)}) copy-start(f32[32,1024]{1,0:T(8,128)} %param.12) | copy-start | bytes 393220
  85.4 71.7 %copy-start = (f32[32,8192]{1,0:T(8,128)}, f32[32,8192]{1,0:T(8,128)S(1)}, u32[]{:S(2)}) copy-start(f32[32,8192]{1,0:T(8,128)S(1)} %fusion.14) | copy-start | bytes 3145732
  111.5 45.6 %copy-start.8 = (f32[32,32]{1,0:T(8,128)}, f32[32,32]{1,0:T(8,128)S(1)}, u32[]{:S(2)}) copy-start(f32[32,32]{1,0:T(8,128)S(1)} %copy.21) | copy-start | bytes 12292
  155.8 1.3 copy-start.5
Sparse Core Ops, SparseCore 0:
  19.8 62.1 all-reduce.4
  115.3 39.5 all-reduce.6
